TPU v7x, 32 devices: a whole 2x2x4 slice. The times are simulated.
32 devices in a mesh: groups: 2 (over y), gy: 4 (over z), gz: 4 (over x, core).
Axes of the slice: x: 2, y: 2, z: 4, core: 2. Of those that a mesh axis runs over, the one named last changes fastest.
Arguments:
- indirect: float32 [4, 512, 32, 512], P('groups', 'gy', 'gz'), parts along dimension 0, may hold values from -6 to 6
- past_indirect: float32 [8, 2, 512, 32, 512], P('groups', None, 'gy', 'gz'), parts along dimension 0, may hold values from -6 to 6
- past_residual: float32 [8, 2, 512, 32, 512], P('groups', None, 'gy', 'gz'), parts along dimension 0, may hold values from -40 to 40
- atom_table: float32 [10, 4, 4, 128], P('groups', 'gy', 'gz'), parts along dimension 0, may hold values from -4 to 512, as said below
- atom_counts: int32 [8, 4], P(('groups', 'gy'), 'gz'), parts along dimension 0, may hold values from 1 to 128, as said below
- chi_amps: float32 [3, 4], replicated, may hold values from -3 to 3
- chi_widths: float32 [4], replicated, may hold values from 0.5 to 4
Outputs:
- new_indirect: float32 [4, 512, 32, 512], P('groups', 'gy', 'gz'), parts along dimension 0
- residual: float32 [4, 512, 32, 512], P('groups', 'gy', 'gz'), parts along dimension 0
There are 2 independent parts, one for each index of `groups`. A program takes and returns all parts, laid end to end along the dimension named above; an argument that names none is the same for every part. Nothing has to cross between parts.
Inputs may be any that keep to these rules, and one draw needn't show every extreme that they name: `atom_counts`: some pencil has exactly 128 live rows in every draw. `atom_table`: each row of pencil (p, q) has its y position in [p * 128, (p + 1) * 128) and its z position in [q * 8, (q + 1) * 8); x positions lie in [0, 512).
All inputs are finite; a program needn't handle non-finite values.
Results may differ from a plain program's by a relative error of at most 0.0003.
Values sent between devices are 32-bit elements; how exact they have to be, the bound alone decides.
A program may use at most 192 MiB of HBM per device.

v0:
```python
import math
import jax
import jax.numpy as jnp
from jax import lax
from jax.sharding import PartitionSpec as P

SIGX = 8
PRECISE = lax.Precision.HIGHEST
MIX_STEP = 0.3
BOND_OH = 1.9
BOND_HH = 3.1


def with_halo(cells, sides, width):
    for axis, dim in sides:
        count = lax.axis_size(axis)
        head = lax.slice_in_dim(cells, 0, width, axis=dim)
        tail = lax.slice_in_dim(cells, cells.shape[dim] - width, cells.shape[dim], axis=dim)
        cells = jnp.concatenate(
            [
                lax.ppermute(tail, axis, [(i, (i + 1) % count) for i in range(count)]),
                cells,
                lax.ppermute(head, axis, [((i + 1) % count, i) for i in range(count)]),
            ],
            axis=dim,
        )
    return cells


def hartley(length):
    position = lax.iota(jnp.int32, length)
    product = position[:, None] * position[None, :] % length
    angle = product.astype(jnp.float32) * (2.0 * math.pi / length)
    return (jnp.cos(angle) + jnp.sin(angle)) / math.sqrt(length)


def wave_squared(position, length):
    folded = jnp.where(2 * position > length, position - length, position)
    scaled = folded.astype(jnp.float32) * (2.0 * math.pi / length)
    return scaled * scaled


def response(wave_square, chi_amps, chi_widths):
    wavenumber = jnp.sqrt(wave_square)
    summed = [jnp.zeros_like(wave_square) for channel in range(3)]
    for which_term in range(chi_widths.shape[0]):
        gaussian_term = jnp.exp(-wave_square * (chi_widths[which_term] * chi_widths[which_term]))
        summed = [
            summed[channel] + chi_amps[channel, which_term] * gaussian_term for channel in range(3)
        ]
    oxygen = 1.0 + summed[0]
    mixed_site = 2.0 * jnp.sinc(wavenumber * (BOND_OH / math.pi)) + summed[1]
    hydrogen = 2.0 + 2.0 * jnp.sinc(wavenumber * (BOND_HH / math.pi)) + summed[2]
    return (oxygen, mixed_site, hydrogen)


def couple(spectrum, wave_square, chi_amps, chi_widths):
    oxygen, mixed_site, hydrogen = response(wave_square, chi_amps, chi_widths)
    return jnp.stack(
        [
            oxygen * spectrum[0] + mixed_site * spectrum[1],
            mixed_site * spectrum[0] + hydrogen * spectrum[1],
        ]
    )


def gaussian(offset, length, spread):
    offset = offset - length * jnp.floor(offset / length + 0.5)
    return jnp.exp(-0.5 * offset * offset / (spread * spread))


def pencil_field(
    atom_rows, pencil_y, pencil_z, cells_y, cells_z, total_x, total_y, total_z, spread_x
):
    cell_y = (pencil_y * cells_y + lax.iota(jnp.int32, cells_y)).astype(jnp.float32)
    cell_z = (pencil_z * cells_z + lax.iota(jnp.int32, cells_z)).astype(jnp.float32)
    cell_x = lax.iota(jnp.int32, total_x).astype(jnp.float32)
    along_y = gaussian(cell_y[:, None] - atom_rows[1][None, :], total_y, 0.5 * cells_y)
    along_z = gaussian(cell_z[:, None] - atom_rows[2][None, :], total_z, 0.5 * cells_z)
    along_x = gaussian(cell_x[:, None] - atom_rows[0][None, :], total_x, spread_x)
    left = atom_rows[3:5][:, None, None, :] * along_y[None, :, None, :] * along_z[None, None, :, :]
    left = left.reshape(2, cells_y * cells_z, atom_rows.shape[1])
    return jnp.einsum("sra,xa->srx", left, along_x, precision=PRECISE)


def body(indirect, past_indirect, past_residual, atom_table, atom_counts, chi_amps, chi_widths):
    cells_y = indirect.shape[1]
    cells_z = indirect.shape[2]
    cells_x = indirect.shape[3]
    parts_y = lax.axis_size("gy")
    parts_z = lax.axis_size("gz")
    total_y = cells_y * parts_y
    total_z = cells_z * parts_z
    row_count = atom_table.shape[3]
    present = (lax.iota(jnp.int32, row_count) < atom_counts[0, 0]).astype(jnp.float32)
    bucket = jnp.concatenate([atom_table[0:3], atom_table[3:5] * present], 0)
    nearby = with_halo(bucket, (("gy", 1), ("gz", 2)), 1)
    nearby = nearby.reshape(5, 9 * row_count)
    potential_field = pencil_field(
        nearby,
        lax.axis_index("gy"),
        lax.axis_index("gz"),
        cells_y,
        cells_z,
        cells_x,
        total_y,
        total_z,
        float(SIGX),
    )
    potential_field = potential_field.reshape(2, cells_y, cells_z, cells_x)
    argument = indirect - potential_field
    closed = jnp.where(argument > 0, argument, jnp.expm1(jnp.minimum(argument, 0.0)))
    direct = closed - indirect
    table_x = hartley(cells_x)
    table_y = hartley(total_y)
    table_z = hartley(total_z)
    blocks = parts_y * parts_z
    width_x = cells_x // blocks
    grid_y = table_y.reshape(parts_y, cells_y, total_y)
    grid_z = table_z.reshape(parts_z, cells_z, total_z)
    outgoing = jnp.einsum(
        "scdx,xqk->sqkdc", direct, table_x.reshape(cells_x, blocks, width_x), precision=PRECISE
    )
    outgoing = outgoing.reshape(2, blocks, 1, width_x * cells_z * cells_y)
    received = lax.all_to_all(outgoing, ("gy", "gz"), split_axis=1, concat_axis=2, tiled=True)
    count = received.shape[0]
    pieces = received.reshape(count, parts_y, parts_z, width_x, cells_z, cells_y)
    partial_value = jnp.einsum("sabxdc,acy->sbxdy", pieces, grid_y, precision=PRECISE)
    section_two = jnp.einsum("sbxdy,bdz->sxzy", partial_value, grid_z, precision=PRECISE)
    wave_x = wave_squared(
        lax.axis_index(("gy", "gz")) * width_x + lax.iota(jnp.int32, width_x), cells_x
    )
    wave_square = (
        wave_x[:, None, None]
        + wave_squared(lax.iota(jnp.int32, total_z), total_z)[None, :, None]
        + wave_squared(lax.iota(jnp.int32, total_y), total_y)[None, None, :]
    )
    coupled = couple(section_two, wave_square, chi_amps, chi_widths)
    partial_value = jnp.einsum("sxzy,bdz->sxbdy", coupled, grid_z, precision=PRECISE)
    returning = jnp.einsum("sxbdy,acy->sabxdc", partial_value, grid_y, precision=PRECISE)
    returning = returning.reshape(2, blocks, 1, width_x * cells_z * cells_y)
    table_back = table_x.reshape(blocks, width_x, cells_x)
    received = lax.all_to_all(returning, ("gy", "gz"), split_axis=1, concat_axis=2, tiled=True)
    count = received.shape[0]
    pieces = received.reshape(count, blocks, width_x, cells_z, cells_y)
    summed_field = jnp.einsum("sqxdc,qxk->scdk", pieces, table_back, precision=PRECISE)
    residual = summed_field - direct - indirect
    stacked = jnp.concatenate([residual[None], past_residual], 0)
    gram_matrix = jnp.einsum("isyzx,jsyzx->ij", stacked, stacked, precision=PRECISE)
    gram_matrix = lax.psum(gram_matrix, ("gy", "gz"))
    factor = jnp.linalg.cholesky(gram_matrix)
    weights = jax.scipy.linalg.cho_solve(
        (factor, True), jnp.ones((gram_matrix.shape[0],), jnp.float32)
    )
    mixing = weights / jnp.sum(weights)
    earlier = jnp.einsum(
        "i,isyzx->syzx", mixing[1:], past_indirect + MIX_STEP * past_residual, precision=PRECISE
    )
    new_indirect = mixing[0] * (indirect + MIX_STEP * residual) + earlier
    return (new_indirect, residual)


def solution(mesh):
    return jax.shard_map(
        body,
        mesh=mesh,
        in_specs=(
            P("groups", "gy", "gz", None),
            P("groups", None, "gy", "gz", None),
            P("groups", None, "gy", "gz", None),
            P("groups", "gy", "gz", None),
            P(("groups", "gy"), "gz"),
            P(),
            P(),
        ),
        out_specs=(P("groups", "gy", "gz", None), P("groups", "gy", "gz", None)),
        check_vma=False,
    )
```

profile of v0, /device:TPU:0, one launch (start us, length us, event | category | flops | bytes accessed | tf_op | source)
XLA Modules:
  0.0 549.4 jit_solution(14519221556603764568)
XLA Ops:
  2.7 3.1 collective-permute-start
  5.7 2.1 collective-permute-start.1
  7.8 1.5 collective-permute-done
  9.4 1.7 collective-permute-start.3
  13.1 18.8 %fusion.6 = f32[2,128,8,512]{3,1,2,0:T(8,128)S(1)} fusion(f32[8,1152]{1,0:T(8,128)S(1)} %fusion.224, f32[2,128,1152]{2,1,0:T(8,128)S(1)} %broadcast_multiply_fusion, f32[1152]{0:T(1024)S(1)} %sub.111, f32[512]{0:T(512)S(1)} %iota_convert_fusion), kind=kOutput, calls=%fused_computation.8 | convolution fusion | flops 14503182336 | bytes 5417472 | tf_op jit(solution)/shard_map/sra,xa->srx/dot_general | solution.py:83
  31.9 14.1 %fusion.56 = f32[2,16,32,8,128]{4,2,3,0,1:T(8,128)S(1)} fusion(f32[2,128,8,512]{3,1,2,0:T(8,128)S(1)} %fusion.6, f32[2,128,8,512]{3,2,1,0:T(8,128)S(1)} %copy-done.2, s32[16,32]{1,0:T(8,128)S(1)} %multiply_add_fusion.3), kind=kOutput, calls=%fused_computation.68 | convolution fusion | flops 6451888128 | bytes 12584960 | tf_op jit(solution)/shard_map/scdx,xqk->sqkdc/dot_general | solution.py:121
  46.0 5.8 %copy.90 = f32[2,16,32,8,128]{4,3,2,0,1:T(8,128)} copy(f32[2,16,32,8,128]{4,2,3,0,1:T(8,128)S(1)} %fusion.56) | data formatting | bytes 8388608 | tf_op jit(solution)/shard_map/reshape | solution.py:124
  51.8 5.9 %reshape.439 = f32[2,16,1,32768]{3,0,2,1:T(2,128)} reshape(f32[2,16,32,8,128]{4,3,2,0,1:T(8,128)} %copy.90) | data formatting | bytes 8388608 | tf_op jit(solution)/shard_map/reshape | solution.py:124
  57.8 6.7 %all-to-all-start = ((f32[2,16,1,32768]{3,0,2,1:T(2,128)}), f32[2,16,1,32768]{3,0,2,1:T(2,128)}, u32[]{:S(2)}, u32[]{:S(2)}) async-start(f32[2,16,1,32768]{3,0,2,1:T(2,128)} %reshape.439), calls=%async_computation | async-start | bytes 8388608 | tf_op jit(solution)/shard_map/all_to_all | solution.py:125
  71.0 71.0 %all-to-all-done = f32[2,16,1,32768]{3,0,2,1:T(2,128)} async-done(((f32[2,16,1,32768]{3,0,2,1:T(2,128)}), f32[2,16,1,32768]{3,0,2,1:T(2,128)}, u32[]{:S(2)}, u32[]{:S(2)}) %all-to-all-start) | async-done | bytes 4194336 | tf_op jit(solution)/shard_map/all_to_all | solution.py:125
  142.1 7.0 %reshape.440 = f32[2,4,4,32,8,128]{5,4,3,0,2,1:T(8,128)} reshape(f32[2,16,1,32768]{3,0,2,1:T(2,128)} %all-to-all-done) | data formatting | bytes 8388608 | tf_op jit(solution)/shard_map/reshape | solution.py:127
  149.1 13.7 %fusion.21 = f32[2,4,32,8,512,1]{4,3,5,1,2,0:T(8,128)S(1)} fusion(f32[2,4,4,32,8,128]{5,4,3,0,2,1:T(8,128)} %reshape.440, s32[4,128]{1,0:T(4,128)S(1)} %multiply_add_fusion.5), kind=kOutput, calls=%fused_computation.26 | convolution fusion | flops 6446645248 | bytes 8390656 | tf_op jit(solution)/shard_map/sabxdc,acy->sbxdy/dot_general | solution.py:128
  162.8 4.3 fusion.59
  167.2 12.9 %fusion.101 = f32[1,32,32,512]{3,2,1,0:T(8,128)S(1)} fusion(f32[2,32,32,512]{3,2,1,0:T(8,128)S(1)} %fusion.59, f32[]{:T(128)} %bitcast.42, f32[]{:T(128)} %bitcast.41, f32[]{:T(128)} %bitcast.40, f32[]{:T(128)} %bitcast.39, f32[]{:T(128)} %bitcast.14, f32[]{:T(128)} %bitcast.12, f32[]{:T(128)} %bitcast.10, f32[]{:T(128)} %bitcast.8, f32[512]{0:T(512)S(1)} %fusion.240, ...), kind=kLoop, calls=%fused_computation.107 | loop fusion | flops 50331648 | bytes 6297648 | tf_op jit(solution)/shard_map/stack | solution.py:59
  180.0 10.3 %fusion.90 = f32[1,32,32,512]{3,2,1,0:T(8,128)S(1)} fusion(f32[2,32,32,512]{3,2,1,0:T(8,128)S(1)} %fusion.59, f32[]{:T(128)} %bitcast.14, f32[]{:T(128)} %bitcast.13, f32[]{:T(128)} %bitcast.12, f32[]{:T(128)} %bitcast.11, f32[]{:T(128)} %bitcast.10, f32[]{:T(128)} %bitcast.9, f32[]{:T(128)} %bitcast.8, f32[512]{0:T(512)S(1)} %fusion.240, ...), kind=kLoop, calls=%fused_computation.96 | loop fusion | flops 31457280 | bytes 6297648 | tf_op jit(solution)/shard_map/stack | solution.py:59
  190.4 4.1 fusion.62
  194.5 13.6 %fusion.63 = f32[2,4,4,32,8,128]{5,3,4,2,0,1:T(8,128)S(1)} fusion(f32[2,32,4,8,512]{4,3,1,0,2:T(8,128)S(1)} %fusion.62, s32[4,128]{1,0:T(4,128)S(1)} %multiply_add_fusion.5), kind=kOutput, calls=%fused_computation.71 | convolution fusion | flops 6446645248 | bytes 8390656 | tf_op jit(solution)/shard_map/sxbdy,acy->sabxdc/dot_general | solution.py:140
  208.0 5.8 %copy.93 = f32[2,4,4,32,8,128]{5,4,3,0,2,1:T(8,128)} copy(f32[2,4,4,32,8,128]{5,3,4,2,0,1:T(8,128)S(1)} %fusion.63) | data formatting | bytes 8388608 | tf_op jit(solution)/shard_map/reshape | solution.py:141
  213.8 5.9 %reshape.441 = f32[2,16,1,32768]{3,0,2,1:T(2,128)} reshape(f32[2,4,4,32,8,128]{5,4,3,0,2,1:T(8,128)} %copy.93) | data formatting | bytes 8388608 | tf_op jit(solution)/shard_map/reshape | solution.py:141
  219.7 19.7 %all-to-all-start.1 = ((f32[2,16,1,32768]{3,0,2,1:T(2,128)}), f32[2,16,1,32768]{3,0,2,1:T(2,128)}, u32[]{:S(2)}, u32[]{:S(2)}) async-start(f32[2,16,1,32768]{3,0,2,1:T(2,128)} %reshape.441), calls=%async_computation.1 | async-start | bytes 8388608 | tf_op jit(solution)/shard_map/all_to_all | solution.py:143
  239.4 18.3 %copy.69 = f32[4,2,128,8,512]{2,0,3,4,1:T(4,128)} copy(f32[4,2,128,8,512]{4,3,2,1,0:T(8,128)} %param.10) | data formatting | bytes 33554432 | tf_op args[2]
  257.7 17.5 %multiply_add_fusion = f32[4,2,128,8,512]{4,3,2,1,0:T(8,128)} fusion(f32[4,2,128,8,512]{4,3,2,1,0:T(8,128)} %param.9, f32[4,2,128,8,512]{4,3,2,1,0:T(8,128)} %param.10), kind=kLoop, calls=%fused_computation.6 | loop fusion | flops 8388608 | bytes 50331648 | tf_op jit(solution)/shard_map/add | solution.py:157
  275.2 41.7 %all-to-all-done.1 = f32[2,16,1,32768]{3,0,2,1:T(2,128)} async-done(((f32[2,16,1,32768]{3,0,2,1:T(2,128)}), f32[2,16,1,32768]{3,0,2,1:T(2,128)}, u32[]{:S(2)}, u32[]{:S(2)}) %all-to-all-start.1) | async-done | bytes 4194336 | tf_op jit(solution)/shard_map/all_to_all | solution.py:143
  317.0 6.6 %reshape.442 = f32[2,16,32,8,128]{4,3,2,0,1:T(8,128)} reshape(f32[2,16,1,32768]{3,0,2,1:T(2,128)} %all-to-all-done.1) | data formatting | bytes 8388608 | tf_op jit(solution)/shard_map/reshape | solution.py:145
  323.6 26.4 %fusion.14 = f32[2,128,8,512]{3,1,2,0:T(8,128)S(1)} fusion(f32[2,128,8,512]{3,2,1,0:T(8,128)} %param.8, f32[2,128,8,512]{3,1,2,0:T(8,128)} %copy-done.6, f32[2,16,32,8,128]{4,3,2,0,1:T(8,128)} %reshape.442, s32[16,32]{1,0:T(8,128)S(1)} %multiply_add_fusion.3), kind=kOutput, calls=%fused_computation.18 | convolution fusion | flops 6453985280 | bytes 16779264 | tf_op jit(solution)/shard_map/sqxdc,qxk->scdk/dot_general | solution.py:146
  350.0 4.4 copy.75
  354.4 11.0 %copy.68 = f32[1,2,128,8,512]{2,0,3,4,1:T(1,128)} copy(f32[1,2,128,8,512]{4,2,3,1,0:T(8,128)} %bitcast.155) | data formatting | bytes 8388608 | tf_op jit(solution)/shard_map/broadcast_in_dim | solution.py:148
  365.4 76.1 %fusion.132 = f32[5,5]{0,1:T(8,128)S(1)} fusion(f32[4,2,128,8,512]{2,0,3,4,1:T(4,128)} %copy.69, f32[1,2,128,8,512]{2,0,3,4,1:T(1,128)} %copy.68), kind=kOutput, calls=%fused_computation.158 | convolution fusion | flops 319815680 | bytes 20971620 | tf_op jit(solution)/shard_map/isyzx,jsyzx->ij/dot_general | solution.py:149
  441.5 47.8 %psum.7 = f32[5,5]{0,1:T(8,128)S(1)} all-reduce(f32[5,5]{0,1:T(8,128)S(1)} %fusion.132), channel_id=1, replica_groups=mesh['groups'=2,'gy'=4,'gz'=4] {'gy','gz'}, use_global_device_ids=true, to_apply=%region_0.2 | all-reduce | flops 25 | bytes 200 | tf_op jit(solution)/shard_map/psum | solution.py:150
  492.8 46.8 %fusion.4 = f32[1,2,128,8,512]{4,0,3,2,1:T(1,128)S(1)} fusion(f32[4,2,128,8,512]{4,3,2,1,0:T(8,128)} %multiply_add_fusion, f32[5]{0:T(128)S(1)} %broadcast_divide_fusion), kind=kOutput, calls=%fused_computation.4 | convolution fusion | flops 50331648 | bytes 20971540 | tf_op jit(solution)/shard_map/i,isyzx->syzx/dot_general | solution.py:156
  539.6 5.1 bitcast_add_fusion
  544.8 4.4 copy.74
  (54 shorter events, 8.4 us)
Async XLA Ops:
  2.7 6.7 %collective-permute-start = (f32[5,1,1,128]{3,2,1,0:T(1,128)S(1)}, f32[5,1,1,128]{3,2,1,0:T(1,128)S(1)}, u32[]{:S(2)}, u32[]{:S(2)}) collective-permute-start(f32[5,1,1,128]{3,2,1,0:T(1,128)S(1)} %pad_maximum_fusion.5), channel_id=1, source_target_pairs={{0,4},{4,8},{8,12},{12,0},{1,5},{5,9},{9,13},{13,1},{2,6},{6,10},{... | collective-permute-start | bytes 7688 | tf_op jit(solution)/shard_map/ppermute | solution.py:21
  5.7 3.6 collective-permute-start.1
  9.3 3.1 collective-permute-start.2
  9.4 3.1 collective-permute-start.3
  13.1 18.8 %copy-start.2 = (f32[2,128,8,512]{3,2,1,0:T(8,128)S(1)}, f32[2,128,8,512]{3,2,1,0:T(8,128)}, u32[]{:S(2)}) copy-start(f32[2,128,8,512]{3,2,1,0:T(8,128)} %param.8) | copy-start | bytes 12582916
  31.9 14.1 %copy-start.6 = (f32[2,128,8,512]{3,1,2,0:T(8,128)}, f32[2,128,8,512]{3,1,2,0:T(8,128)S(1)}, u32[]{:S(2)}) copy-start(f32[2,128,8,512]{3,1,2,0:T(8,128)S(1)} %fusion.6) | copy-start | bytes 12582916
  57.7 6.8 %copy-start.5 = (f32[4]{0:T(128)S(1)}, f32[4]{0:T(128)}, u32[]{:S(2)}) copy-start(f32[4]{0:T(128)} %param.14) | copy-start | bytes 52
  57.8 12.5 %copy-start.4 = (f32[3,4]{1,0:T(4,128)S(1)}, f32[3,4]{1,0:T(4,128)}, u32[]{:S(2)}) copy-start(f32[3,4]{1,0:T(4,128)} %param.13) | copy-start | bytes 148
  57.8 84.3 %all-to-all-start = ((f32[2,16,1,32768]{3,0,2,1:T(2,128)}), f32[2,16,1,32768]{3,0,2,1:T(2,128)}, u32[]{:S(2)}, u32[]{:S(2)}) async-start(f32[2,16,1,32768]{3,0,2,1:T(2,128)} %reshape.439), calls=%async_computation | async-start | bytes 8388608 | tf_op jit(solution)/shard_map/all_to_all | solution.py:125
  219.7 97.2 %all-to-all-start.1 = ((f32[2,16,1,32768]{3,0,2,1:T(2,128)}), f32[2,16,1,32768]{3,0,2,1:T(2,128)}, u32[]{:S(2)}, u32[]{:S(2)}) async-start(f32[2,16,1,32768]{3,0,2,1:T(2,128)} %reshape.441), calls=%async_computation.1 | async-start | bytes 8388608 | tf_op jit(solution)/shard_map/all_to_all | solution.py:143
  350.0 4.5 copy-start
  492.8 46.8 %copy-start.1 = (f32[2,128,8,512]{3,1,2,0:T(8,128)S(1)}, f32[2,128,8,512]{3,1,2,0:T(8,128)}, u32[]{:S(2)}) copy-start(f32[2,128,8,512]{3,1,2,0:T(8,128)} %copy-done) | copy-start | bytes 12582916
  492.8 46.8 %copy-start.3 = (f32[2,128,8,512]{3,2,1,0:T(8,128)S(1)}, f32[2,128,8,512]{3,2,1,0:T(8,128)}, u32[]{:S(2)}) copy-start(f32[2,128,8,512]{3,2,1,0:T(8,128)} %param.8) | copy-start | bytes 12582916
where the time goes:
time: 558 us; the launch traced here: 549 us
  matrix products  219 us (39%)
  waiting for transfers between devices  116 us (21%)
  local copies, waits for them, and re-layouts  77.4 us (14%)
  other arithmetic  49.8 us (9%)
  blocking collectives  47.8 us (9%)
  starting transfers between devices  33.4 us (6%)
  between operations  6.84 us (1%)
    dot_general x1, matrix products, body(): jnp.einsum('isyzx,jsyzx->ij', stacked, stacked, precision=PRECISE)  76.1 us
    all_to_all x1, waiting for transfers between devices, body(): lax.all_to_all(outgoing, ('gy', 'gz'), split_axis=1, concat_axis=2, tiled...  71 us
    psum x1, blocking collectives, body(): gram_matrix = lax.psum(gram_matrix, ('gy', 'gz'))  47.8 us
    dot_general x1, matrix products, body(): jnp.einsum('i,isyzx->syzx', mixing[1:], past_indirect + MIX_STEP * past_r...  46.8 us
    all_to_all x1, waiting for transfers between devices, body(): lax.all_to_all(returning, ('gy', 'gz'), split_axis=1, concat_axis=2, tile...  41.7 us
    unnamed x17, local copies, waits for them, and re-layouts  27.2 us
    dot_general x1, matrix products, body(): jnp.einsum('sqxdc,qxk->scdk', pieces, table_back, precision=PRECISE)  26.4 us
    another operation x2, other arithmetic, couple(): jnp.stack([oxygen * spectrum[0] + mixed_site * spectrum[1], mixed_site *...  23.2 us
  transfers between devices with their start and end apart: 6, of which 4 were waited for; matrix products, arithmetic and copies ran while one was open for 7% of the time, Pallas kernels for 0%

commit v1 on v0

--- a/solution.py
+++ b/solution.py
@@ -9,6 +9,29 @@
 MIX_STEP = 0.3
 BOND_OH = 1.9
 BOND_HH = 3.1
+
+
+def split_up(value, dim, length):
+    shape = value.shape
+    tiles = value.reshape(*shape[:dim], length, shape[dim] // length, *shape[dim + 1 :])
+    return jnp.moveaxis(tiles, dim, 0)
+
+
+def joined_along(pieces, dim):
+    lengths = list(pieces.shape[1:])
+    lengths[dim] *= pieces.shape[0]
+    return jnp.moveaxis(pieces, 0, dim).reshape(lengths)
+
+
+def exchange_in_pairs(x, axis, split_dim, concat_dim):
+    count, index = (lax.axis_size(axis), lax.axis_index(axis))
+    parts = split_up(x, split_dim, count)
+    done = [parts[index]]
+    for step in range(1, count):
+        sent = parts[index ^ step]
+        done.append(lax.ppermute(sent, axis, [(i, i ^ step) for i in range(count)]))
+    parts = jnp.stack(done)[index ^ jnp.arange(count)]
+    return joined_along(parts, concat_dim)
 
 
 def with_halo(cells, sides, width):
@@ -140,7 +163,7 @@
     returning = jnp.einsum("sxbdy,acy->sabxdc", partial_value, grid_y, precision=PRECISE)
     returning = returning.reshape(2, blocks, 1, width_x * cells_z * cells_y)
     table_back = table_x.reshape(blocks, width_x, cells_x)
-    received = lax.all_to_all(returning, ("gy", "gz"), split_axis=1, concat_axis=2, tiled=True)
+    received = exchange_in_pairs(returning, ("gy", "gz"), 1, 2)
     count = received.shape[0]
     pieces = received.reshape(count, blocks, width_x, cells_z, cells_y)
     summed_field = jnp.einsum("sqxdc,qxk->scdk", pieces, table_back, precision=PRECISE)

time: 558 us -> 587 us (1.052)
  waiting for transfers between devices: 116 us -> 71.3 us
  local copies, waits for them, and re-layouts: 77.4 us -> 116 us
  starting transfers between devices: 33.4 us -> 68.1 us
    ppermute x0 -> x15, starting transfers between devices: none -> 54.4 us  [exchange_in_pairs(): done.append(lax.ppermute(sent, axis, [(i, i ^ step) for i in range(count)]))]
    all_to_all x1 -> x0, waiting for transfers between devices: 41.7 us -> none  [body(): lax.all_to_all(returning, ('gy', 'gz'), split_axis=1, concat_axis=2, tile...]
    all_to_all x1, waiting for transfers between devices: 71 us -> 35.1 us  [body(): lax.all_to_all(outgoing, ('gy', 'gz'), split_axis=1, concat_axis=2, tiled...]
    ppermute x0 -> x15, waiting for transfers between devices: none -> 33.4 us  [exchange_in_pairs(): done.append(lax.ppermute(sent, axis, [(i, i ^ step) for i in range(count)]))]
    another operation x0 -> x4, local copies, waits for them, and re-layouts: none -> 29.1 us
    all_to_all x1 -> x0, starting transfers between devices: 19.7 us -> none  [body(): lax.all_to_all(returning, ('gy', 'gz'), split_axis=1, concat_axis=2, tile...]
    reshape x3 -> x0, local copies, waits for them, and re-layouts: 18.3 us -> none  [the longest x2 11.7 us: body(): returning = returning.reshape(2, blocks, 1, width_x * cells_z * cells_y)]
    unnamed x17 -> x47, local copies, waits for them, and re-layouts: 27.2 us -> 41.3 us
  transfers between devices with their start and end apart: 6 -> 20, of which waited for: 4 -> 8; matrix products, arithmetic and copies ran while one was open for 7% -> 9% of each run, Pallas kernels for 0% -> 0%
where the time goes in v1:
time: 587 us; the launch traced here: 579 us
  matrix products  219 us (37%)
  local copies, waits for them, and re-layouts  116 us (20%)
  waiting for transfers between devices  71.3 us (12%)
  starting transfers between devices  68.1 us (12%)
  other arithmetic  50.3 us (9%)
  blocking collectives  46.4 us (8%)
  between operations  7.31 us (1%)
    dot_general x1, matrix products, body(): jnp.einsum('isyzx,jsyzx->ij', stacked, stacked, precision=PRECISE)  76.1 us
    ppermute x15, starting transfers between devices, exchange_in_pairs(): done.append(lax.ppermute(sent, axis, [(i, i ^ step) for i in range(count)]))  54.4 us
    dot_general x1, matrix products, body(): jnp.einsum('i,isyzx->syzx', mixing[1:], past_indirect + MIX_STEP * past_r...  46.6 us
    psum x1, blocking collectives, body(): gram_matrix = lax.psum(gram_matrix, ('gy', 'gz'))  46.4 us
    unnamed x47, local copies, waits for them, and re-layouts  41.3 us
    all_to_all x1, waiting for transfers between devices, body(): lax.all_to_all(outgoing, ('gy', 'gz'), split_axis=1, concat_axis=2, tiled...  35.1 us
    ppermute x15, waiting for transfers between devices, exchange_in_pairs(): done.append(lax.ppermute(sent, axis, [(i, i ^ step) for i in range(count)]))  33.4 us
    dot_general x1, matrix products, body(): jnp.einsum('sqxdc,qxk->scdk', pieces, table_back, precision=PRECISE)  26.6 us
  transfers between devices with their start and end apart: 20, of which 8 were waited for; matrix products, arithmetic and copies ran while one was open for 9% of the time, Pallas kernels for 0%

profile of v1, /device:TPU:0, one launch (start us, length us, event | category | flops | bytes accessed | tf_op | source)
XLA Modules:
  0.0 578.9 jit_solution(2546400152684250464)
XLA Ops:
  13.1 18.8 %fusion.6 = f32[2,128,8,512]{3,1,2,0:T(8,128)S(1)} fusion(f32[8,1152]{1,0:T(8,128)S(1)} %fusion.224, f32[2,128,1152]{2,1,0:T(8,128)S(1)} %broadcast_multiply_fusion, f32[1152]{0:T(1024)S(1)} %sub.111, f32[512]{0:T(512)S(1)} %iota_convert_fusion), kind=kOutput, calls=%fused_computation.9 | convolution fusion | flops 14503182336 | bytes 5417472 | tf_op jit(solution)/shard_map/sra,xa->srx/dot_general | solution.py:106
  32.0 14.3 %fusion.56 = f32[2,16,32,8,128]{4,2,3,0,1:T(8,128)S(1)} fusion(f32[2,128,8,512]{3,1,2,0:T(8,128)S(1)} %fusion.6, f32[2,128,8,512]{3,2,1,0:T(8,128)S(1)} %copy-done.2, s32[16,32]{1,0:T(8,128)S(1)} %multiply_add_fusion.3), kind=kOutput, calls=%fused_computation.69 | convolution fusion | flops 6451888128 | bytes 12584960 | tf_op jit(solution)/shard_map/scdx,xqk->sqkdc/dot_general | solution.py:144
  46.3 5.8 %copy.105 = f32[2,16,32,8,128]{4,3,2,0,1:T(8,128)} copy(f32[2,16,32,8,128]{4,2,3,0,1:T(8,128)S(1)} %fusion.56) | data formatting | bytes 8388608 | tf_op jit(solution)/shard_map/reshape | solution.py:147
  52.1 5.9 %reshape.488 = f32[2,16,1,32768]{3,0,2,1:T(2,128)} reshape(f32[2,16,32,8,128]{4,3,2,0,1:T(8,128)} %copy.105) | data formatting | bytes 8388608 | tf_op jit(solution)/shard_map/reshape | solution.py:147
  58.0 6.8 %all-to-all-start = ((f32[2,16,1,32768]{3,0,2,1:T(2,128)}), f32[2,16,1,32768]{3,0,2,1:T(2,128)}, u32[]{:S(2)}, u32[]{:S(2)}) async-start(f32[2,16,1,32768]{3,0,2,1:T(2,128)} %reshape.488), calls=%async_computation | async-start | bytes 8388608 | tf_op jit(solution)/shard_map/all_to_all | solution.py:148
  70.6 18.3 %copy.84 = f32[4,2,128,8,512]{2,0,3,4,1:T(4,128)} copy(f32[4,2,128,8,512]{4,3,2,1,0:T(8,128)} %param.10) | data formatting | bytes 33554432 | tf_op args[2]
  89.7 17.5 %multiply_add_fusion = f32[4,2,128,8,512]{4,3,2,1,0:T(8,128)} fusion(f32[4,2,128,8,512]{4,3,2,1,0:T(8,128)} %param.9, f32[4,2,128,8,512]{4,3,2,1,0:T(8,128)} %param.10), kind=kLoop, calls=%fused_computation.7 | loop fusion | flops 8388608 | bytes 50331648 | tf_op jit(solution)/shard_map/add | solution.py:180
  107.2 35.1 %all-to-all-done = f32[2,16,1,32768]{3,0,2,1:T(2,128)} async-done(((f32[2,16,1,32768]{3,0,2,1:T(2,128)}), f32[2,16,1,32768]{3,0,2,1:T(2,128)}, u32[]{:S(2)}, u32[]{:S(2)}) %all-to-all-start) | async-done | bytes 4194336 | tf_op jit(solution)/shard_map/all_to_all | solution.py:148
  142.3 6.8 %reshape.489 = f32[2,4,4,32,8,128]{5,4,3,0,2,1:T(8,128)} reshape(f32[2,16,1,32768]{3,0,2,1:T(2,128)} %all-to-all-done) | data formatting | bytes 8388608 | tf_op jit(solution)/shard_map/reshape | solution.py:150
  149.1 13.7 %fusion.21 = f32[2,4,32,8,512,1]{4,3,5,1,2,0:T(8,128)S(1)} fusion(f32[2,4,4,32,8,128]{5,4,3,0,2,1:T(8,128)} %reshape.489, s32[4,128]{1,0:T(4,128)S(1)} %multiply_add_fusion.5), kind=kOutput, calls=%fused_computation.27 | convolution fusion | flops 6446645248 | bytes 8390656 | tf_op jit(solution)/shard_map/sabxdc,acy->sbxdy/dot_general | solution.py:151
  162.8 4.5 fusion.59
  167.4 12.9 %fusion.101 = f32[1,32,32,512]{3,2,1,0:T(8,128)S(1)} fusion(f32[2,32,32,512]{3,2,1,0:T(8,128)S(1)} %fusion.59, f32[]{:T(128)} %bitcast.42, f32[]{:T(128)} %bitcast.41, f32[]{:T(128)} %bitcast.40, f32[]{:T(128)} %bitcast.39, f32[]{:T(128)} %bitcast.14, f32[]{:T(128)} %bitcast.12, f32[]{:T(128)} %bitcast.10, f32[]{:T(128)} %bitcast.8, f32[512]{0:T(512)S(1)} %fusion.246, ...), kind=kLoop, calls=%fused_computation.108 | loop fusion | flops 50331648 | bytes 6297648 | tf_op jit(solution)/shard_map/stack | solution.py:82
  180.2 10.6 %fusion.90 = f32[1,32,32,512]{3,2,1,0:T(8,128)S(1)} fusion(f32[2,32,32,512]{3,2,1,0:T(8,128)S(1)} %fusion.59, f32[]{:T(128)} %bitcast.14, f32[]{:T(128)} %bitcast.13, f32[]{:T(128)} %bitcast.12, f32[]{:T(128)} %bitcast.11, f32[]{:T(128)} %bitcast.10, f32[]{:T(128)} %bitcast.9, f32[]{:T(128)} %bitcast.8, f32[512]{0:T(512)S(1)} %fusion.246, ...), kind=kLoop, calls=%fused_computation.97 | loop fusion | flops 31457280 | bytes 6297648 | tf_op jit(solution)/shard_map/stack | solution.py:82
  195.0 13.3 %fusion.63 = f32[2,4,4,32,8,128]{5,3,4,2,0,1:T(8,128)S(1)} fusion(f32[2,32,4,8,512]{4,3,1,0,2:T(8,128)S(1)} %fusion.62, s32[4,128]{1,0:T(4,128)S(1)} %multiply_add_fusion.5), kind=kOutput, calls=%fused_computation.72 | convolution fusion | flops 6446645248 | bytes 8390656 | tf_op jit(solution)/shard_map/sxbdy,acy->sabxdc/dot_general | solution.py:163
  208.3 5.8 %copy.78 = f32[2,4,4,32,8,128]{5,4,3,2,1,0:T(8,128)} copy(f32[2,4,4,32,8,128]{5,3,4,2,0,1:T(8,128)S(1)} %fusion.63) | data formatting | bytes 8388608 | tf_op jit(solution)/shard_map/sxbdy,acy->sabxdc/transpose | solution.py:163
  214.1 5.0 reshape_reshape.6
  219.1 16.8 %constant_dynamic-slice_fusion = (f32[2,1,1,1,32768]{4,1,0,3,2:T(1,128)S(1)}, f32[2,1,1,1,32768]{4,1,0,3,2:T(1,128)S(1)}, f32[2,1,1,1,32768]{4,1,0,3,2:T(1,128)S...) fusion(f32[2,16,1,1,32768]{4,1,0,3,2:T(8,128)} %reshape_reshape, ...), kind=kLoop, calls=%fused_computation.309 | loop fusion | bytes 8388672 | tf_op jit(solution)/shard_map/dynamic-slice.15
  238.2 6.3 %collective-permute-start.5 = (f32[2,1,1,32768]{3,0,2,1:T(2,128)S(1)}, f32[2,1,1,32768]{3,0,2,1:T(2,128)S(1)}, u32[]{:S(2)}, u32[]{:S(2)}) collective-permute-start(f32[2,1,1,32768]{3,0,2,1:T(2,128)S(1)} %bitcast.251), channel_id=1, source_target_pairs={{0,2},{1,3},{2,0},{3,1},{4,6},{5,7},{6,4},{7,5},{8,10},{9,11},{10,... | collective-permute-start | bytes 786440 | tf_op jit(solution)/shard_map/ppermute | solution.py:32
  245.0 11.3 %collective-permute-start.7 = (f32[2,1,1,32768]{3,0,2,1:T(2,128)S(1)}, f32[2,1,1,32768]{3,0,2,1:T(2,128)S(1)}, u32[]{:S(2)}, u32[]{:S(2)}) collective-permute-start(f32[2,1,1,32768]{3,0,2,1:T(2,128)S(1)} %bitcast.249), channel_id=1, source_target_pairs={{0,4},{1,5},{2,6},{3,7},{4,0},{5,1},{6,2},{7,3},{8,12},{9,13},{10,... | collective-permute-start | bytes 786440 | tf_op jit(solution)/shard_map/ppermute | solution.py:32
  263.1 6.0 %collective-permute-start.11 = (f32[2,1,1,32768]{3,0,2,1:T(2,128)S(1)}, f32[2,1,1,32768]{3,0,2,1:T(2,128)S(1)}, u32[]{:S(2)}, u32[]{:S(2)}) collective-permute-start(f32[2,1,1,32768]{3,0,2,1:T(2,128)S(1)} %bitcast.245), channel_id=1, source_target_pairs={{0,8},{1,9},{2,10},{3,11},{4,12},{5,13},{6,14},{7,15},{8,0},{9,1},... | collective-permute-start | bytes 786440 | tf_op jit(solution)/shard_map/ppermute | solution.py:32
  273.8 13.5 %collective-permute-done.9 = f32[2,1,1,32768]{3,0,2,1:T(2,128)S(1)} collective-permute-done((f32[2,1,1,32768]{3,0,2,1:T(2,128)S(1)}, f32[2,1,1,32768]{3,0,2,1:T(2,128)S(1)}, u32[]{:S(2)}, u32[]{:S(2)}) %collective-permute-start.9) | collective-permute-done | bytes 262176 | tf_op jit(solution)/shard_map/ppermute | solution.py:32
  288.1 4.9 collective-permute-done.10
  297.7 20.9 %collective-permute-start.17 = (f32[2,1,1,32768]{3,0,2,1:T(2,128)S(1)}, f32[2,1,1,32768]{3,0,2,1:T(2,128)S(1)}, u32[]{:S(2)}, u32[]{:S(2)}) collective-permute-start(f32[2,1,1,32768]{3,0,2,1:T(2,128)S(1)} %bitcast.239), channel_id=1, source_target_pairs={{0,14},{1,15},{2,12},{3,13},{4,10},{5,11},{6,8},{7,9},{8,6},{9,7},... | collective-permute-start | bytes 786440 | tf_op jit(solution)/shard_map/ppermute | solution.py:32
  319.3 7.6 %collective-permute-done.13 = f32[2,1,1,32768]{3,0,2,1:T(2,128)S(1)} collective-permute-done((f32[2,1,1,32768]{3,0,2,1:T(2,128)S(1)}, f32[2,1,1,32768]{3,0,2,1:T(2,128)S(1)}, u32[]{:S(2)}, u32[]{:S(2)}) %collective-permute-start.13) | collective-permute-done | bytes 262176 | tf_op jit(solution)/shard_map/ppermute | solution.py:32
  338.5 8.6 %gather_fusion = f32[16,2,32768]{2,1,0:T(2,128)} fusion(f32[16,2,32768]{2,1,0:T(2,128)} %bitcast.63, s32[1024]{0:T(1024)S(1)} %pad_clamp_fusion), kind=kCustom, calls=%fused_computation | custom fusion | bytes 8388672 | tf_op jit(solution)/shard_map/gather | solution.py:33
  347.1 6.6 %reshape.490 = f32[2,16,32,8,128]{4,3,2,0,1:T(8,128)} reshape(f32[2,1,16,1,32768]{4,0,2,3,1:T(2,128)} %bitcast.237) | data formatting | bytes 8388608 | tf_op jit(solution)/shard_map/reshape;reshape | solution.py:168
  353.7 26.6 %fusion.14 = f32[2,128,8,512]{3,1,2,0:T(8,128)S(1)} fusion(f32[2,128,8,512]{3,2,1,0:T(8,128)} %param.8, f32[2,128,8,512]{3,1,2,0:T(8,128)} %copy-done.6, f32[2,16,32,8,128]{4,3,2,0,1:T(8,128)} %reshape.490, s32[16,32]{1,0:T(8,128)S(1)} %multiply_add_fusion.3), kind=kOutput, calls=%fused_computation.19 | convolution fusion | flops 6453985280 | bytes 16779264 | tf_op jit(solution)/shard_map/sqxdc,qxk->scdk/dot_general | solution.py:169
  384.8 11.0 %copy.83 = f32[1,2,128,8,512]{2,0,3,4,1:T(1,128)} copy(f32[1,2,128,8,512]{4,2,3,1,0:T(8,128)} %bitcast.236) | data formatting | bytes 8388608 | tf_op jit(solution)/shard_map/broadcast_in_dim | solution.py:171
  395.8 76.1 %fusion.132 = f32[5,5]{0,1:T(8,128)S(1)} fusion(f32[4,2,128,8,512]{2,0,3,4,1:T(4,128)} %copy.84, f32[1,2,128,8,512]{2,0,3,4,1:T(1,128)} %copy.83), kind=kOutput, calls=%fused_computation.159 | convolution fusion | flops 319815680 | bytes 20971620 | tf_op jit(solution)/shard_map/isyzx,jsyzx->ij/dot_general | solution.py:172
  471.9 46.4 %psum.7 = f32[5,5]{0,1:T(8,128)S(1)} all-reduce(f32[5,5]{0,1:T(8,128)S(1)} %fusion.132), channel_id=1, replica_groups=mesh['groups'=2,'gy'=4,'gz'=4] {'gy','gz'}, use_global_device_ids=true, to_apply=%region_0.2 | all-reduce | flops 25 | bytes 200 | tf_op jit(solution)/shard_map/psum | solution.py:173
  522.2 46.6 %fusion.4 = f32[1,2,128,8,512]{4,0,3,2,1:T(1,128)S(1)} fusion(f32[4,2,128,8,512]{4,3,2,1,0:T(8,128)} %multiply_add_fusion, f32[5]{0:T(128)S(1)} %broadcast_divide_fusion), kind=kOutput, calls=%fused_computation.5 | convolution fusion | flops 50331648 | bytes 20971540 | tf_op jit(solution)/shard_map/i,isyzx->syzx/dot_general | solution.py:179
  568.8 5.1 bitcast_add_fusion
  (117 shorter events, 62.1 us)
Async XLA Ops:
  2.7 6.7 %collective-permute-start = (f32[5,1,1,128]{3,2,1,0:T(1,128)S(1)}, f32[5,1,1,128]{3,2,1,0:T(1,128)S(1)}, u32[]{:S(2)}, u32[]{:S(2)}) collective-permute-start(f32[5,1,1,128]{3,2,1,0:T(1,128)S(1)} %pad_maximum_fusion.5), channel_id=1, source_target_pairs={{0,4},{4,8},{8,12},{12,0},{1,5},{5,9},{9,13},{13,1},{2,6},{6,10},{... | collective-permute-start | bytes 7688 | tf_op jit(solution)/shard_map/ppermute | solution.py:44
  5.7 3.6 collective-permute-start.1
  9.3 3.1 collective-permute-start.2
  9.4 3.1 collective-permute-start.3
  13.1 18.8 %copy-start.2 = (f32[2,128,8,512]{3,2,1,0:T(8,128)S(1)}, f32[2,128,8,512]{3,2,1,0:T(8,128)}, u32[]{:S(2)}) copy-start(f32[2,128,8,512]{3,2,1,0:T(8,128)} %param.8) | copy-start | bytes 12582916
  32.0 14.3 %copy-start.6 = (f32[2,128,8,512]{3,1,2,0:T(8,128)}, f32[2,128,8,512]{3,1,2,0:T(8,128)S(1)}, u32[]{:S(2)}) copy-start(f32[2,128,8,512]{3,1,2,0:T(8,128)S(1)} %fusion.6) | copy-start | bytes 12582916
  58.0 6.8 %copy-start.5 = (f32[4]{0:T(128)S(1)}, f32[4]{0:T(128)}, u32[]{:S(2)}) copy-start(f32[4]{0:T(128)} %param.14) | copy-start | bytes 52
  58.0 84.3 %all-to-all-start = ((f32[2,16,1,32768]{3,0,2,1:T(2,128)}), f32[2,16,1,32768]{3,0,2,1:T(2,128)}, u32[]{:S(2)}, u32[]{:S(2)}) async-start(f32[2,16,1,32768]{3,0,2,1:T(2,128)} %reshape.488), calls=%async_computation | async-start | bytes 8388608 | tf_op jit(solution)/shard_map/all_to_all | solution.py:148
  70.5 18.4 %copy-start.4 = (f32[3,4]{1,0:T(4,128)S(1)}, f32[3,4]{1,0:T(4,128)}, u32[]{:S(2)}) copy-start(f32[3,4]{1,0:T(4,128)} %param.13) | copy-start | bytes 148
  236.1 22.6 %collective-permute-start.4 = (f32[2,1,1,32768]{3,0,2,1:T(2,128)S(1)}, f32[2,1,1,32768]{3,0,2,1:T(2,128)S(1)}, u32[]{:S(2)}, u32[]{:S(2)}) collective-permute-start(f32[2,1,1,32768]{3,0,2,1:T(2,128)S(1)} %bitcast.252), channel_id=1, source_target_pairs={{0,1},{1,0},{2,3},{3,2},{4,5},{5,4},{6,7},{7,6},{8,9},{9,8},{10,11... | collective-permute-start | bytes 786440 | tf_op jit(solution)/shard_map/ppermute | solution.py:32
  238.2 24.1 %collective-permute-start.5 = (f32[2,1,1,32768]{3,0,2,1:T(2,128)S(1)}, f32[2,1,1,32768]{3,0,2,1:T(2,128)S(1)}, u32[]{:S(2)}, u32[]{:S(2)}) collective-permute-start(f32[2,1,1,32768]{3,0,2,1:T(2,128)S(1)} %bitcast.251), channel_id=1, source_target_pairs={{0,2},{1,3},{2,0},{3,1},{4,6},{5,7},{6,4},{7,5},{8,10},{9,11},{10,... | collective-permute-start | bytes 786440 | tf_op jit(solution)/shard_map/ppermute | solution.py:32
  244.7 18.4 %collective-permute-start.6 = (f32[2,1,1,32768]{3,0,2,1:T(2,128)S(1)}, f32[2,1,1,32768]{3,0,2,1:T(2,128)S(1)}, u32[]{:S(2)}, u32[]{:S(2)}) collective-permute-start(f32[2,1,1,32768]{3,0,2,1:T(2,128)S(1)} %bitcast.250), channel_id=1, source_target_pairs={{0,3},{1,2},{2,1},{3,0},{4,7},{5,6},{6,5},{7,4},{8,11},{9,10},{10,... | collective-permute-start | bytes 786440 | tf_op jit(solution)/shard_map/ppermute | solution.py:32
  245.0 24.8 %collective-permute-start.7 = (f32[2,1,1,32768]{3,0,2,1:T(2,128)S(1)}, f32[2,1,1,32768]{3,0,2,1:T(2,128)S(1)}, u32[]{:S(2)}, u32[]{:S(2)}) collective-permute-start(f32[2,1,1,32768]{3,0,2,1:T(2,128)S(1)} %bitcast.249), channel_id=1, source_target_pairs={{0,4},{1,5},{2,6},{3,7},{4,0},{5,1},{6,2},{7,3},{8,12},{9,13},{10,... | collective-permute-start | bytes 786440 | tf_op jit(solution)/shard_map/ppermute | solution.py:32
  256.5 14.3 %collective-permute-start.8 = (f32[2,1,1,32768]{3,0,2,1:T(2,128)S(1)}, f32[2,1,1,32768]{3,0,2,1:T(2,128)S(1)}, u32[]{:S(2)}, u32[]{:S(2)}) collective-permute-start(f32[2,1,1,32768]{3,0,2,1:T(2,128)S(1)} %bitcast.248), channel_id=1, source_target_pairs={{0,5},{1,4},{2,7},{3,6},{4,1},{5,0},{6,3},{7,2},{8,13},{9,12},{10,... | collective-permute-start | bytes 786440 | tf_op jit(solution)/shard_map/ppermute | solution.py:32
  258.7 28.7 %collective-permute-start.9 = (f32[2,1,1,32768]{3,0,2,1:T(2,128)S(1)}, f32[2,1,1,32768]{3,0,2,1:T(2,128)S(1)}, u32[]{:S(2)}, u32[]{:S(2)}) collective-permute-start(f32[2,1,1,32768]{3,0,2,1:T(2,128)S(1)} %bitcast.247), channel_id=1, source_target_pairs={{0,6},{1,7},{2,4},{3,5},{4,2},{5,3},{6,0},{7,1},{8,14},{9,15},{10,... | collective-permute-start | bytes 786440 | tf_op jit(solution)/shard_map/ppermute | solution.py:32
  262.4 30.6 %collective-permute-start.10 = (f32[2,1,1,32768]{3,0,2,1:T(2,128)S(1)}, f32[2,1,1,32768]{3,0,2,1:T(2,128)S(1)}, u32[]{:S(2)}, u32[]{:S(2)}) collective-permute-start(f32[2,1,1,32768]{3,0,2,1:T(2,128)S(1)} %bitcast.246), channel_id=1, source_target_pairs={{0,7},{1,6},{2,5},{3,4},{4,3},{5,2},{6,1},{7,0},{8,15},{9,14},{10,... | collective-permute-start | bytes 786440 | tf_op jit(solution)/shard_map/ppermute | solution.py:32
  263.1 32.3 %collective-permute-start.11 = (f32[2,1,1,32768]{3,0,2,1:T(2,128)S(1)}, f32[2,1,1,32768]{3,0,2,1:T(2,128)S(1)}, u32[]{:S(2)}, u32[]{:S(2)}) collective-permute-start(f32[2,1,1,32768]{3,0,2,1:T(2,128)S(1)} %bitcast.245), channel_id=1, source_target_pairs={{0,8},{1,9},{2,10},{3,11},{4,12},{5,13},{6,14},{7,15},{8,0},{9,1},... | collective-permute-start | bytes 786440 | tf_op jit(solution)/shard_map/ppermute | solution.py:32
  269.8 27.9 %collective-permute-start.12 = (f32[2,1,1,32768]{3,0,2,1:T(2,128)S(1)}, f32[2,1,1,32768]{3,0,2,1:T(2,128)S(1)}, u32[]{:S(2)}, u32[]{:S(2)}) collective-permute-start(f32[2,1,1,32768]{3,0,2,1:T(2,128)S(1)} %bitcast.244), channel_id=1, source_target_pairs={{0,9},{1,8},{2,11},{3,10},{4,13},{5,12},{6,15},{7,14},{8,1},{9,0},... | collective-permute-start | bytes 786440 | tf_op jit(solution)/shard_map/ppermute | solution.py:32
  270.7 56.1 %collective-permute-start.13 = (f32[2,1,1,32768]{3,0,2,1:T(2,128)S(1)}, f32[2,1,1,32768]{3,0,2,1:T(2,128)S(1)}, u32[]{:S(2)}, u32[]{:S(2)}) collective-permute-start(f32[2,1,1,32768]{3,0,2,1:T(2,128)S(1)} %bitcast.243), channel_id=1, source_target_pairs={{0,10},{1,11},{2,8},{3,9},{4,14},{5,15},{6,12},{7,13},{8,2},{9,3},... | collective-permute-start | bytes 786440 | tf_op jit(solution)/shard_map/ppermute | solution.py:32
  287.4 44.4 %collective-permute-start.14 = (f32[2,1,1,32768]{3,0,2,1:T(2,128)S(1)}, f32[2,1,1,32768]{3,0,2,1:T(2,128)S(1)}, u32[]{:S(2)}, u32[]{:S(2)}) collective-permute-start(f32[2,1,1,32768]{3,0,2,1:T(2,128)S(1)} %bitcast.242), channel_id=1, source_target_pairs={{0,11},{1,10},{2,9},{3,8},{4,15},{5,14},{6,13},{7,12},{8,3},{9,2},... | collective-permute-start | bytes 786440 | tf_op jit(solution)/shard_map/ppermute | solution.py:32
  293.0 39.5 %collective-permute-start.15 = (f32[2,1,1,32768]{3,0,2,1:T(2,128)S(1)}, f32[2,1,1,32768]{3,0,2,1:T(2,128)S(1)}, u32[]{:S(2)}, u32[]{:S(2)}) collective-permute-start(f32[2,1,1,32768]{3,0,2,1:T(2,128)S(1)} %bitcast.241), channel_id=1, source_target_pairs={{0,12},{1,13},{2,14},{3,15},{4,8},{5,9},{6,10},{7,11},{8,4},{9,5},... | collective-permute-start | bytes 786440 | tf_op jit(solution)/shard_map/ppermute | solution.py:32
  295.4 37.8 %collective-permute-start.16 = (f32[2,1,1,32768]{3,0,2,1:T(2,128)S(1)}, f32[2,1,1,32768]{3,0,2,1:T(2,128)S(1)}, u32[]{:S(2)}, u32[]{:S(2)}) collective-permute-start(f32[2,1,1,32768]{3,0,2,1:T(2,128)S(1)} %bitcast.240), channel_id=1, source_target_pairs={{0,13},{1,12},{2,15},{3,14},{4,9},{5,8},{6,11},{7,10},{8,5},{9,4},... | collective-permute-start | bytes 786440 | tf_op jit(solution)/shard_map/ppermute | solution.py:32
  297.7 36.2 %collective-permute-start.17 = (f32[2,1,1,32768]{3,0,2,1:T(2,128)S(1)}, f32[2,1,1,32768]{3,0,2,1:T(2,128)S(1)}, u32[]{:S(2)}, u32[]{:S(2)}) collective-permute-start(f32[2,1,1,32768]{3,0,2,1:T(2,128)S(1)} %bitcast.239), channel_id=1, source_target_pairs={{0,14},{1,15},{2,12},{3,13},{4,10},{5,11},{6,8},{7,9},{8,6},{9,7},... | collective-permute-start | bytes 786440 | tf_op jit(solution)/shard_map/ppermute | solution.py:32
  326.9 10.9 %collective-permute-start.18 = (f32[2,1,1,32768]{3,0,2,1:T(2,128)S(1)}, f32[2,1,1,32768]{3,0,2,1:T(2,128)S(1)}, u32[]{:S(2)}, u32[]{:S(2)}) collective-permute-start(f32[2,1,1,32768]{3,0,2,1:T(2,128)S(1)} %bitcast.238), channel_id=1, source_target_pairs={{0,15},{1,14},{2,13},{3,12},{4,11},{5,10},{6,9},{7,8},{8,7},{9,6},... | collective-permute-start | bytes 786440 | tf_op jit(solution)/shard_map/ppermute | solution.py:32
  380.3 4.5 copy-start
  522.2 46.7 %copy-start.1 = (f32[2,128,8,512]{3,1,2,0:T(8,128)S(1)}, f32[2,128,8,512]{3,1,2,0:T(8,128)}, u32[]{:S(2)}) copy-start(f32[2,128,8,512]{3,1,2,0:T(8,128)} %copy-done) | copy-start | bytes 12582916
  522.2 46.7 %copy-start.3 = (f32[2,128,8,512]{3,2,1,0:T(8,128)S(1)}, f32[2,128,8,512]{3,2,1,0:T(8,128)}, u32[]{:S(2)}) copy-start(f32[2,128,8,512]{3,2,1,0:T(8,128)} %param.8) | copy-start | bytes 12582916
